TPU v7x, 128 devices: a whole 4x4x4 slice. The times are simulated.
128 devices in a mesh: replica: 16 (over x_lo, z, core), tensor: 8 (over y, x_hi).
Axes of the slice: x: 4 (x_hi: 2, x_lo: 2; x = x_hi * 2 + x_lo), y: 4, z: 4, core: 2. Of those that a mesh axis runs over, the one named last changes fastest.
Arguments:
- tokens: bfloat16 [8192, 1024], P('replica'), may hold values from -6 to 6
- targets: bfloat16 [8192, 1024], P('replica'), may hold values from -6 to 6
- row_ids: int32 [16, 3, 512], P('replica'), may hold values from 0 to 511
- anchor: float32 [2, 1024, 4096], P(None, None, 'tensor'), may hold values from -0.1875 to 0.1875
- momentum: float32 [16, 2, 1024, 4096], P('replica', None, None, 'tensor'), may hold values from -4 to 4
- slow: float32 [2, 1024, 4096], P(None, None, 'tensor'), may hold values from -6 to 6
Outputs:
- anchor_new: float32 [2, 1024, 4096], P(None, None, 'tensor')
- slow_new: float32 [2, 1024, 4096], P(None, None, 'tensor')
- momentum_new: float32 [16, 2, 1024, 4096], P('replica', None, None, 'tensor')
Inputs may be any that keep to these rules, and one draw needn't show every extreme that they name: `row_ids`: each id names a row within its replica's own block of 512 rows; rows may repeat.
All inputs are finite; a program needn't handle non-finite values.
Results may differ from a plain program's by a relative error of at most 0.008.
Values may be sent and summed in bfloat16 or wider, within the bound.
A program may use at most 128 MiB of HBM per device.

v0:
```python
import jax
import jax.numpy as jnp
from jax import lax
from jax.sharding import PartitionSpec as P

INNER = 3
learn_rate = 0.02
inner_beta = 0.9
slow_beta = 0.5


def passed_along(block, axis, distance):
    devices = range(lax.axis_size(axis))
    route = [((i - distance) % len(devices), i) for i in devices]
    return lax.ppermute(block, axis, route)


def gelu_pair(pre):
    coeff = 0.7978845608028654
    inner = coeff * (pre + 0.044715 * pre * pre * pre)
    tanh_val = jnp.tanh(inner)
    value = 0.5 * pre * (1.0 + tanh_val)
    slope = 0.5 * (1.0 + tanh_val) + 0.5 * pre * (1.0 - tanh_val * tanh_val) * coeff * (
        1.0 + 3.0 * 0.044715 * pre * pre
    )
    return (value, slope)


def body(tokens, targets, row_ids, anchor, momentum, slow):
    row_count = tokens.shape[0]
    scale = 1.0 / row_count
    weights = anchor
    moment = momentum[0]
    parts = lax.axis_size("tensor")
    own = lax.axis_index("tensor")
    shard_rows = row_count // parts
    for step in range(INNER):
        if step > 0:
            incoming = passed_along(weights.astype(jnp.bfloat16), "replica", 2 ** (step - 1))
            weights = 0.5 * (weights + incoming.astype(jnp.float32))
        picks = row_ids[0, step]
        inputs = jnp.take(tokens, picks, axis=0)
        own_picks = lax.dynamic_slice(picks, (own * shard_rows,), (shard_rows,))
        wanted = jnp.take(targets, own_picks, axis=0)
        weights_bf = weights.astype(jnp.bfloat16)
        pre = jnp.dot(inputs, weights_bf[0], preferred_element_type=jnp.float32)
        value, slope = gelu_pair(pre)
        hidden = value.astype(jnp.bfloat16)
        partial_out = lax.dot_general(
            hidden, weights_bf[1], (((1,), (1,)), ((), ())), preferred_element_type=jnp.float32
        ).astype(jnp.bfloat16)
        summed = lax.psum_scatter(partial_out, "tensor", scatter_dimension=0, tiled=True)
        error = ((summed.astype(jnp.float32) - wanted.astype(jnp.float32)) * scale).astype(
            jnp.bfloat16
        )
        error = lax.all_gather(error, "tensor", axis=0, tiled=True)
        back = (jnp.dot(error, weights_bf[1], preferred_element_type=jnp.float32) * slope).astype(
            jnp.bfloat16
        )
        grad_in = lax.dot_general(
            inputs, back, (((0,), (0,)), ((), ())), preferred_element_type=jnp.float32
        )
        grad_out = lax.dot_general(
            error, hidden, (((0,), (0,)), ((), ())), preferred_element_type=jnp.float32
        )
        moment = inner_beta * moment + jnp.stack([grad_in, grad_out])
        weights = weights - learn_rate * moment
    replicas = lax.axis_size("replica")
    moved = ((anchor - weights) / learn_rate).astype(jnp.bfloat16)
    total = lax.psum_scatter(moved, "replica", scatter_dimension=1, tiled=True)
    total = lax.all_gather(total, "replica", axis=1, tiled=True)
    slow_new = slow_beta * slow + total.astype(jnp.float32) / replicas
    anchor_new = anchor - learn_rate * slow_new
    return (anchor_new, slow_new, moment[None])


def solution(mesh):
    return jax.shard_map(
        body,
        mesh=mesh,
        in_specs=(
            P("replica", None),
            P("replica", None),
            P("replica", None, None),
            P(None, None, "tensor"),
            P("replica", None, None, "tensor"),
            P(None, None, "tensor"),
        ),
        out_specs=(
            P(None, None, "tensor"),
            P(None, None, "tensor"),
            P("replica", None, None, "tensor"),
        ),
        check_vma=False,
    )
```

profile of v0, /device:TPU:1, one launch (start us, length us, event | category | flops | bytes accessed | tf_op | source)
XLA Modules:
  0.0 628.3 jit_solution(16959371402139294303)
XLA Ops:
  7.2 0.8 fusion.106
  8.1 2.5 convert_element_type.81
  10.5 2.8 gather_fusion
  13.3 2.0 fusion.37
  15.3 1.0 copy-done.19
  16.3 3.1 convolution_convert_fusion.2
  19.6 0.7 gather_fusion.1
  20.3 72.9 %reduce-scatter.5.cloned.1.call-done = bf16[64,1024]{1,0:T(8,128)(2,1)} async-done(((bf16[512,1024]{1,0:T(8,128)(2,1)}), bf16[64,1024]{1,0:T(8,128)(2,1)}) %reduce-scatter.5.cloned.1.call-update) | async-done | bytes 131088 | tf_op jit(solution)/shard_map/reduce_scatter | solution.py:52
  93.2 1.7 multiply_convert_fusion.5
  95.0 46.8 %all-gather.5.cloned.1.call-done = bf16[512,1024]{1,0:T(8,128)(2,1)} async-done(((bf16[64,1024]{1,0:T(8,128)(2,1)}), bf16[512,1024]{1,0:T(8,128)(2,1)}) %all-gather.5.cloned.1.call-update) | async-done | bytes 1048592 | tf_op jit(solution)/shard_map/all_gather | solution.py:56
  141.8 3.9 fusion.16
  145.7 3.2 fusion.102
  149.2 7.0 %fusion.86 = (bf16[2,1024,512]{2,1,0:T(8,128)(2,1)}, f32[2,1024,512]{2,1,0:T(8,128)}) fusion(f32[2,1024,512]{2,1,0:T(8,128)S(1)} %copy-done.2, f32[1,1024,512]{2,1,0:T(8,128)S(1)} %bitcast.73, f32[1,1024,512]{2,1,0:T(8,128)S(1)} %bitcast.71, f32[1,2,1024,512]{3,2,1,0:T(8,128)} %param.14), kind=kLoop, calls=%fused_computation.144 | loop fusion | flops 6291456 | bytes 18874368 | tf_op jit(solution)/shard_map/convert_element_type | solution.py:39
  156.2 3.4 collective-permute-start
  159.7 2.8 gather_fusion.2
  162.5 20.5 %collective-permute-done = bf16[2,1024,512]{2,1,0:T(8,128)(2,1)S(1)} collective-permute-done((bf16[2,1024,512]{2,1,0:T(8,128)(2,1)}, bf16[2,1024,512]{2,1,0:T(8,128)(2,1)S(1)}, u32[]{:S(2)}, u32[]{:S(2)}) %collective-permute-start) | collective-permute-done | bytes 2097184 | tf_op jit(solution)/shard_map/ppermute | solution.py:15
  183.0 5.5 fusion.9
  188.5 0.8 fusion.36
  189.3 0.6 copy-done.15
  189.8 1.0 copy-done.21
  190.8 1.8 convolution_convert_fusion.1
  192.8 0.7 gather_fusion.3
  193.5 69.1 %reduce-scatter.7.cloned.1.call-done = bf16[64,1024]{1,0:T(8,128)(2,1)} async-done(((bf16[512,1024]{1,0:T(8,128)(2,1)}), bf16[64,1024]{1,0:T(8,128)(2,1)}) %reduce-scatter.7.cloned.1.call-update) | async-done | bytes 131088 | tf_op jit(solution)/shard_map/reduce_scatter | solution.py:52
  262.5 1.7 multiply_convert_fusion.4
  264.5 45.9 %all-gather.7.cloned.1.call-done = bf16[512,1024]{1,0:T(8,128)(2,1)} async-done(((bf16[64,1024]{1,0:T(8,128)(2,1)}), bf16[512,1024]{1,0:T(8,128)(2,1)}) %all-gather.7.cloned.1.call-update) | async-done | bytes 1048592 | tf_op jit(solution)/shard_map/all_gather | solution.py:56
  310.4 3.9 fusion.15
  314.3 2.5 fusion.103
  317.1 5.2 fusion.105
  322.3 1.3 collective-permute-start.1
  323.6 2.8 gather_fusion.4
  326.4 43.2 %collective-permute-done.1 = bf16[2,1024,512]{2,1,0:T(8,128)(2,1)} collective-permute-done((bf16[2,1024,512]{2,1,0:T(8,128)(2,1)}, bf16[2,1024,512]{2,1,0:T(8,128)(2,1)}, u32[]{:S(2)}, u32[]{:S(2)}) %collective-permute-start.1) | collective-permute-done | bytes 2097184 | tf_op jit(solution)/shard_map/ppermute | solution.py:15
  369.7 6.3 %fusion.10 = bf16[2,1024,512]{2,1,0:T(8,128)(2,1)S(1)} fusion(bf16[2,1024,512]{2,1,0:T(8,128)(2,1)} %collective-permute-done.1, f32[1,1024,512]{2,1,0:T(8,128)} %bitcast.68, f32[1,1024,512]{2,1,0:T(8,128)S(1)} %bitcast.64, f32[2,1024,512]{2,1,0:T(8,128)} %get-tuple-element.12, bf16[2,1024,512]{2,1,0:T(8,128)(2,1)} %copy-done.6, f32[2,1024,512]{2,1,0:T(8,128)} %param.13), kind=kLoop, calls=%fused_computation.26 | loop fusion | flops 14680064 | bytes 18874368 | tf_op jit(solution)/shard_map/convert_element_type | solution.py:45
  376.0 0.8 fusion.35
  376.7 0.6 copy-done.14
  377.3 1.0 copy-done.20
  378.3 1.8 convolution_convert_fusion
  380.2 0.7 gather_fusion.5
  380.9 68.4 %reduce-scatter.9.cloned.1.call-done = bf16[64,1024]{1,0:T(8,128)(2,1)} async-done(((bf16[512,1024]{1,0:T(8,128)(2,1)}), bf16[64,1024]{1,0:T(8,128)(2,1)}) %reduce-scatter.9.cloned.1.call-update) | async-done | bytes 131088 | tf_op jit(solution)/shard_map/reduce_scatter | solution.py:52
  449.3 1.7 multiply_convert_fusion.3
  451.1 46.2 %all-gather.9.cloned.1.call-done = bf16[512,1024]{1,0:T(8,128)(2,1)} async-done(((bf16[64,1024]{1,0:T(8,128)(2,1)}), bf16[512,1024]{1,0:T(8,128)(2,1)}) %all-gather.9.cloned.1.call-update) | async-done | bytes 1048592 | tf_op jit(solution)/shard_map/all_gather | solution.py:56
  497.3 5.3 fusion.14
  502.6 2.2 fusion.104
  504.9 1.3 copy-done.12
  506.2 6.9 %fusion.4 = bf16[2,1024,512]{2,1,0:T(8,128)(2,1)} fusion(f32[2,1024,512]{2,1,0:T(8,128)S(1)} %copy-done.4, f32[1,1024,512]{2,1,0:T(8,128)S(1)} %bitcast.77, f32[1,1024,512]{2,1,0:T(8,128)} %bitcast.75, bf16[2,1024,512]{2,1,0:T(8,128)(2,1)} %collective-permute-done.1, f32[1,1024,512]{2,1,0:T(8,128)} %bitcast.69, f32[1,1024,512]{2,1,0:T(8,128)S(1)} %bitcast.65, ...), kind=kLoop, calls=%fused_computation.13 | loop fusion | flops 22020096 | bytes 23068672 | tf_op jit(solution)/shard_map/convert_element_type | solution.py:69
  513.4 60.7 %reduce-scatter.11.cloned.1.call-done = bf16[2,64,512]{2,1,0:T(8,128)(2,1)} async-done(((bf16[2,1024,512]{2,1,0:T(8,128)(2,1)}), bf16[2,64,512]{2,1,0:T(8,128)(2,1)}) %reduce-scatter.11.cloned.1.call-update) | async-done | bytes 131088 | tf_op jit(solution)/shard_map/reduce_scatter | solution.py:70
  574.1 7.7 %fusion.8 = f32[1,2,1024,512]{3,2,1,0:T(8,128)} fusion(f32[1,1,1024,512]{3,2,1,0:T(8,128)} %bitcast.74, f32[1,1,1024,512]{3,2,1,0:T(8,128)} %bitcast.72, f32[1,1,1024,512]{3,2,1,0:T(8,128)} %bitcast.70, f32[1,1,1024,512]{3,2,1,0:T(8,128)S(1)} %bitcast.66, f32[1,1,1024,512]{3,2,1,0:T(8,128)} %bitcast.78, f32[1,1,1024,512]{3,2,1,0:T(8,128)} %bitcast.76, ...), kind=kLoop, calls=%fused_computation.18 | loop fusion | flops 9437184 | bytes 20971520 | tf_op jit(solution)/shard_map/add | solution.py:66
  581.8 30.7 %all-gather.11.cloned.1.call-done = bf16[2,1024,512]{2,1,0:T(8,128)(2,1)} async-done(((bf16[2,64,512]{2,1,0:T(8,128)(2,1)}), bf16[2,1024,512]{2,1,0:T(8,128)(2,1)}) %all-gather.11.cloned.1.call-update) | async-done | bytes 2097168 | tf_op jit(solution)/shard_map/all_gather | solution.py:71
  612.5 9.0 %multiply_subtract_fusion = (f32[2,1024,512]{2,1,0:T(8,128)}, f32[2,1024,512]{2,1,0:T(8,128)}) fusion(f32[2,1024,512]{2,1,0:T(8,128)} %param.13, bf16[2,1024,512]{2,1,0:T(8,128)(2,1)} %all-gather.11.cloned.1.call-done, f32[2,1024,512]{2,1,0:T(8,128)} %param.15), kind=kLoop, calls=%fused_computation.19 | loop fusion | flops 6291456 | bytes 18874368 | tf_op jit(solution)/shard_map/sub | solution.py:73
  (69 shorter events, 1.9 us)
Async XLA Ops:
  7.2 3.4 copy-start
  7.2 86.0 %reduce-scatter.5.cloned.1.call-start = ((), (), s32[]{:S(2)}) async-start(), calls=%async_computation.4 | async-start | bytes 1179648 | tf_op jit(solution)/shard_map/reduce_scatter | solution.py:52
  10.5 2.8 copy-start.13
  15.3 1.0 copy-start.19
  16.3 3.3 copy-start.7
  19.4 122.3 %all-gather.5.cloned.1.call-start = ((), (), s32[]{:S(2)}) async-start(), calls=%async_computation.5 | async-start | bytes 1179648 | tf_op jit(solution)/shard_map/all_gather | solution.py:56
  94.9 167.6 %reduce-scatter.7.cloned.1.call-start = ((), (), s32[]{:S(2)}) async-start(), calls=%async_computation.6 | async-start | bytes 1179648 | tf_op jit(solution)/shard_map/reduce_scatter | solution.py:52
  145.7 10.6 %copy-start.10 = (f32[1024,512]{1,0:T(8,128)}, f32[1024,512]{1,0:T(8,128)S(1)}, u32[]{:S(2)}) copy-start(f32[1024,512]{1,0:T(8,128)S(1)} %fusion.16) | copy-start | bytes 6291460
  145.7 3.6 copy-start.2
  148.9 7.3 %copy-start.11 = (f32[1024,512]{1,0:T(8,128)}, f32[1024,512]{1,0:T(8,128)S(1)}, u32[]{:S(2)}) copy-start(f32[1024,512]{1,0:T(8,128)S(1)} %fusion.102) | copy-start | bytes 6291460
  156.2 26.7 %collective-permute-start = (bf16[2,1024,512]{2,1,0:T(8,128)(2,1)}, bf16[2,1024,512]{2,1,0:T(8,128)(2,1)S(1)}, u32[]{:S(2)}, u32[]{:S(2)}) collective-permute-start(bf16[2,1024,512]{2,1,0:T(8,128)(2,1)} %get-tuple-element.11), channel_id=1, source_target_pairs={{120,0},{0,8},{8,16},{16,24},{24,32},{32,40},{40,48},{48,56},{56,6... | collective-permute-start | bytes 6291464 | tf_op jit(solution)/shard_map/ppermute | solution.py:15
  183.0 5.5 copy-start.6
  183.0 5.5 copy-start.16
  188.5 1.3 copy-start.15
  189.8 1.0 copy-start.21
  190.8 1.9 copy-start.8
  192.6 117.8 %all-gather.7.cloned.1.call-start = ((), (), s32[]{:S(2)}) async-start(), calls=%async_computation.7 | async-start | bytes 1179648 | tf_op jit(solution)/shard_map/all_gather | solution.py:56
  264.2 185.1 %reduce-scatter.9.cloned.1.call-start = ((), (), s32[]{:S(2)}) async-start(), calls=%async_computation.8 | async-start | bytes 1179648 | tf_op jit(solution)/shard_map/reduce_scatter | solution.py:52
  314.3 2.8 copy-start.3
  316.9 5.4 copy-start.5
  322.3 47.3 %collective-permute-start.1 = (bf16[2,1024,512]{2,1,0:T(8,128)(2,1)}, bf16[2,1024,512]{2,1,0:T(8,128)(2,1)}, u32[]{:S(2)}, u32[]{:S(2)}) collective-permute-start(bf16[2,1024,512]{2,1,0:T(8,128)(2,1)} %fusion.105), channel_id=1, source_target_pairs={{112,0},{120,8},{0,16},{8,24},{16,32},{24,40},{32,48},{40,56},{48,... | collective-permute-start | bytes 6291464 | tf_op jit(solution)/shard_map/ppermute | solution.py:15
  326.4 49.5 %copy-start.17 = (bf16[512,1024]{1,0:T(8,128)(2,1)S(1)}, bf16[512,1024]{1,0:T(8,128)(2,1)}, u32[]{:S(2)}) copy-start(bf16[512,1024]{1,0:T(8,128)(2,1)} %gather_fusion.4) | copy-start | bytes 3145732
  376.0 1.3 copy-start.14
  377.3 1.0 copy-start.20
  378.3 1.9 copy-start.9
  380.1 117.2 %all-gather.9.cloned.1.call-start = ((), (), s32[]{:S(2)}) async-start(), calls=%async_computation.9 | async-start | bytes 1179648 | tf_op jit(solution)/shard_map/all_gather | solution.py:56
  451.0 123.1 %reduce-scatter.11.cloned.1.call-start = ((), (), s32[]{:S(2)}) async-start(), calls=%async_computation.10 | async-start | bytes 2228224 | tf_op jit(solution)/shard_map/reduce_scatter | solution.py:70
  497.2 5.3 copy-start.18
  502.6 3.6 copy-start.4
  504.8 1.3 copy-start.12
  513.1 99.4 %all-gather.11.cloned.1.call-start = ((), (), s32[]{:S(2)}) async-start(), calls=%async_computation.11 | async-start | bytes 2228224 | tf_op jit(solution)/shard_map/all_gather | solution.py:71
  612.5 9.0 %copy-start.1 = (bf16[512,1024]{1,0:T(8,128)(2,1)S(1)}, bf16[512,1024]{1,0:T(8,128)(2,1)}, u32[]{:S(2)}) copy-start(bf16[512,1024]{1,0:T(8,128)(2,1)} %param.10) | copy-start | bytes 3145732
Sparse Core Ops, SparseCore 0:
  19.5 73.6 reduce-scatter.4
  96.1 45.5 all-gather.4
  192.7 69.7 reduce-scatter.6
  264.8 45.6 all-gather.6
  380.2 69.1 reduce-scatter.8
  451.6 45.6 all-gather.8
  513.2 60.8 reduce-scatter.10
  575.8 36.6 all-gather.10
where the time goes:
time: 629 us; the launch traced here: 628 us
  waiting for transfers between devices  505 us (80%)
  other arithmetic  55.4 us (9%)
  matrix products  31.2 us (5%)
  local copies, waits for them, and re-layouts  17.4 us (3%)
  between operations  14.4 us (2%)
    reduce_scatter x3, waiting for transfers between devices, body(): lax.psum_scatter(partial_out, 'tensor', scatter_dimension=0, tiled=True)  210 us
    all_gather x3, waiting for transfers between devices, body(): error = lax.all_gather(error, 'tensor', axis=0, tiled=True)  139 us
    ppermute x2, waiting for transfers between devices, passed_along(): return lax.ppermute(block, axis, route)  63.7 us
    reduce_scatter x1, waiting for transfers between devices, body(): total = lax.psum_scatter(moved, 'replica', scatter_dimension=1, tiled=True)  60.7 us
    all_gather x1, waiting for transfers between devices, body(): total = lax.all_gather(total, 'replica', axis=1, tiled=True)  30.7 us
    convert_element_type x3, other arithmetic, body(): weights_bf = weights.astype(jnp.bfloat16)  14.2 us
    dot_general x3, matrix products, body(): lax.dot_general(inputs, back, (((0,), (0,)), ((), ())), preferred_element...  13.1 us
  transfers between devices with their start and end apart: 10, of which 10 were waited for; matrix products, arithmetic and copies ran while one was open for 2% of the time, Pallas kernels for 0%

commit v1 on v0

--- a/solution.py
+++ b/solution.py
@@ -53,7 +53,10 @@
         error = ((summed.astype(jnp.float32) - wanted.astype(jnp.float32)) * scale).astype(
             jnp.bfloat16
         )
-        error = lax.all_gather(error, "tensor", axis=0, tiled=True)
+        peers = lax.axis_size("tensor")
+        shards = jnp.stack([error for _ in range(peers)])
+        shards = lax.all_to_all(shards, "tensor", split_axis=0, concat_axis=0)
+        error = jnp.concatenate(shards, axis=0)
         back = (jnp.dot(error, weights_bf[1], preferred_element_type=jnp.float32) * slope).astype(
             jnp.bfloat16
         )

time: 629 us -> 543 us (0.86)
  waiting for transfers between devices: 505 us -> 363 us
  blocking collectives: 0 us -> 56.9 us
    all_gather x3 -> x0, waiting for transfers between devices: 139 us -> none  [body(): error = lax.all_gather(error, 'tensor', axis=0, tiled=True)]
    all_to_all x0 -> x3, blocking collectives: none -> 56.9 us  [body(): shards = lax.all_to_all(shards, 'tensor', split_axis=0, concat_axis=0)]
  transfers between devices with their start and end apart: 10 -> 7, of which waited for: 10 -> 7; matrix products, arithmetic and copies ran while one was open for 2% -> 3% of each run, Pallas kernels for 0% -> 0%
where the time goes in v1:
time: 543 us
  waiting for transfers between devices  363 us (67%)
  blocking collectives  56.9 us (10%)
  other arithmetic  53.4 us (10%)
  matrix products  31.3 us (6%)
  local copies, waits for them, and re-layouts  17.7 us (3%)
  between operations  14.1 us (3%)
  starting transfers between devices  6.46 us (1%)
    reduce_scatter x3, waiting for transfers between devices, body(): lax.psum_scatter(partial_out, 'tensor', scatter_dimension=0, tiled=True)  210 us
    ppermute x2, waiting for transfers between devices, passed_along(): return lax.ppermute(block, axis, route)  62.4 us
    reduce_scatter x1, waiting for transfers between devices, body(): total = lax.psum_scatter(moved, 'replica', scatter_dimension=1, tiled=True)  60.7 us
    all_to_all x3, blocking collectives, body(): shards = lax.all_to_all(shards, 'tensor', split_axis=0, concat_axis=0)  56.9 us
    all_gather x1, waiting for transfers between devices, body(): total = lax.all_gather(total, 'replica', axis=1, tiled=True)  30.1 us
    convert_element_type x3, other arithmetic, body(): weights_bf = weights.astype(jnp.bfloat16)  14.2 us
    dot_general x3, matrix products, body(): lax.dot_general(inputs, back, (((0,), (0,)), ((), ())), preferred_element...  13.1 us
    convert_element_type x2, other arithmetic, body(): weights.astype(jnp.bfloat16)  12.2 us
  transfers between devices with their start and end apart: 7, of which 7 were waited for; matrix products, arithmetic and copies ran while one was open for 3% of the time, Pallas kernels for 0%

profile of v1, /device:TPU:1, one launch (start us, length us, event | category | flops | bytes accessed | tf_op | source)
XLA Modules:
  0.0 543.0 jit_solution(10677576147503099453)
XLA Ops:
  7.2 0.8 fusion.106
  8.1 2.5 convert_element_type.81
  10.5 2.8 gather_fusion
  13.3 2.0 fusion.37
  15.3 1.0 copy-done.19
  16.3 3.1 convolution_convert_fusion.2
  19.6 0.7 gather_fusion.1
  20.3 72.9 %reduce-scatter.5.cloned.1.call-done = bf16[64,1024]{1,0:T(8,128)(2,1)} async-done(((bf16[512,1024]{1,0:T(8,128)(2,1)}), bf16[64,1024]{1,0:T(8,128)(2,1)}) %reduce-scatter.5.cloned.1.call-update) | async-done | bytes 131088 | tf_op jit(solution)/shard_map/reduce_scatter | solution.py:52
  93.2 1.0 multiply_convert_fusion.5
  94.3 19.0 %all_to_all.15 = bf16[8,64,1024]{2,1,0:T(8,128)(2,1)} all-to-all(bf16[8,64,1024]{2,1,0:T(8,128)(2,1)S(1)} %stack.78), channel_id=1, replica_groups=mesh['replica'=16,'tensor'=8] {'tensor'}, dimensions={0} | all-to-all | bytes 2097152 | tf_op jit(solution)/shard_map/all_to_all | solution.py:58
  113.3 3.9 fusion.16
  117.2 3.2 fusion.102
  120.8 7.0 %fusion.86 = (bf16[2,1024,512]{2,1,0:T(8,128)(2,1)}, f32[2,1024,512]{2,1,0:T(8,128)}) fusion(f32[2,1024,512]{2,1,0:T(8,128)S(1)} %copy-done.2, f32[1,1024,512]{2,1,0:T(8,128)S(1)} %bitcast.76, f32[1,1024,512]{2,1,0:T(8,128)S(1)} %bitcast.74, f32[1,2,1024,512]{3,2,1,0:T(8,128)} %param.14), kind=kLoop, calls=%fused_computation.144 | loop fusion | flops 6291456 | bytes 18874368 | tf_op jit(solution)/shard_map/convert_element_type | solution.py:39
  127.8 4.7 collective-permute-start
  132.5 2.8 gather_fusion.2
  135.3 20.5 %collective-permute-done = bf16[2,1024,512]{2,1,0:T(8,128)(2,1)S(1)} collective-permute-done((bf16[2,1024,512]{2,1,0:T(8,128)(2,1)}, bf16[2,1024,512]{2,1,0:T(8,128)(2,1)S(1)}, u32[]{:S(2)}, u32[]{:S(2)}) %collective-permute-start) | collective-permute-done | bytes 2097184 | tf_op jit(solution)/shard_map/ppermute | solution.py:15
  155.8 5.5 %fusion.9 = bf16[2,1024,512]{2,1,0:T(8,128)(2,1)S(1)} fusion(bf16[2,1024,512]{2,1,0:T(8,128)(2,1)S(1)} %collective-permute-done, f32[2,1024,512]{2,1,0:T(8,128)} %param.13, f32[2,1024,512]{2,1,0:T(8,128)} %get-tuple-element.12), kind=kLoop, calls=%fused_computation.25 | loop fusion | flops 6291456 | bytes 12582912 | tf_op jit(solution)/shard_map/convert_element_type | solution.py:45
  161.3 0.8 fusion.36
  162.1 0.6 copy-done.15
  162.6 1.0 copy-done.21
  163.6 1.8 convolution_convert_fusion.1
  165.6 0.7 gather_fusion.3
  166.3 67.6 %reduce-scatter.7.cloned.1.call-done = bf16[64,1024]{1,0:T(8,128)(2,1)} async-done(((bf16[512,1024]{1,0:T(8,128)(2,1)}), bf16[64,1024]{1,0:T(8,128)(2,1)}) %reduce-scatter.7.cloned.1.call-update) | async-done | bytes 131088 | tf_op jit(solution)/shard_map/reduce_scatter | solution.py:52
  233.9 1.0 multiply_convert_fusion.4
  235.0 19.0 %all_to_all.16 = bf16[8,64,1024]{2,1,0:T(8,128)(2,1)} all-to-all(bf16[8,64,1024]{2,1,0:T(8,128)(2,1)S(1)} %stack.82), channel_id=1, replica_groups=mesh['replica'=16,'tensor'=8] {'tensor'}, dimensions={0} | all-to-all | bytes 2097152 | tf_op jit(solution)/shard_map/all_to_all | solution.py:58
  254.0 3.9 fusion.15
  257.9 2.5 fusion.103
  260.7 5.2 fusion.105
  265.9 1.3 collective-permute-start.1
  267.2 2.8 gather_fusion.4
  270.1 41.9 %collective-permute-done.1 = bf16[2,1024,512]{2,1,0:T(8,128)(2,1)} collective-permute-done((bf16[2,1024,512]{2,1,0:T(8,128)(2,1)}, bf16[2,1024,512]{2,1,0:T(8,128)(2,1)}, u32[]{:S(2)}, u32[]{:S(2)}) %collective-permute-start.1) | collective-permute-done | bytes 2097184 | tf_op jit(solution)/shard_map/ppermute | solution.py:15
  312.0 6.3 %fusion.10 = bf16[2,1024,512]{2,1,0:T(8,128)(2,1)S(1)} fusion(bf16[2,1024,512]{2,1,0:T(8,128)(2,1)} %collective-permute-done.1, f32[1,1024,512]{2,1,0:T(8,128)} %bitcast.71, f32[1,1024,512]{2,1,0:T(8,128)S(1)} %bitcast.67, f32[2,1024,512]{2,1,0:T(8,128)} %get-tuple-element.12, bf16[2,1024,512]{2,1,0:T(8,128)(2,1)} %copy-done.6, f32[2,1024,512]{2,1,0:T(8,128)} %param.13), kind=kLoop, calls=%fused_computation.26 | loop fusion | flops 14680064 | bytes 18874368 | tf_op jit(solution)/shard_map/convert_element_type | solution.py:45
  318.3 0.8 fusion.35
  319.0 0.6 copy-done.14
  319.6 1.0 copy-done.20
  320.6 1.8 convolution_convert_fusion
  322.6 0.7 gather_fusion.5
  323.3 69.4 %reduce-scatter.9.cloned.1.call-done = bf16[64,1024]{1,0:T(8,128)(2,1)} async-done(((bf16[512,1024]{1,0:T(8,128)(2,1)}), bf16[64,1024]{1,0:T(8,128)(2,1)}) %reduce-scatter.9.cloned.1.call-update) | async-done | bytes 131088 | tf_op jit(solution)/shard_map/reduce_scatter | solution.py:52
  392.7 1.0 multiply_convert_fusion.3
  393.9 19.0 %all_to_all.17 = bf16[8,64,1024]{2,1,0:T(8,128)(2,1)} all-to-all(bf16[8,64,1024]{2,1,0:T(8,128)(2,1)S(1)} %stack.86), channel_id=1, replica_groups=mesh['replica'=16,'tensor'=8] {'tensor'}, dimensions={0} | all-to-all | bytes 2097152 | tf_op jit(solution)/shard_map/all_to_all | solution.py:58
  412.9 5.3 fusion.14
  418.2 2.2 fusion.104
  420.4 1.3 copy-done.12
  421.8 6.9 %fusion.4 = bf16[2,1024,512]{2,1,0:T(8,128)(2,1)} fusion(f32[2,1024,512]{2,1,0:T(8,128)S(1)} %copy-done.4, f32[1,1024,512]{2,1,0:T(8,128)S(1)} %bitcast.80, f32[1,1024,512]{2,1,0:T(8,128)} %bitcast.78, bf16[2,1024,512]{2,1,0:T(8,128)(2,1)} %collective-permute-done.1, f32[1,1024,512]{2,1,0:T(8,128)} %bitcast.72, f32[1,1024,512]{2,1,0:T(8,128)S(1)} %bitcast.68, ...), kind=kLoop, calls=%fused_computation.13 | loop fusion | flops 22020096 | bytes 23068672 | tf_op jit(solution)/shard_map/convert_element_type | solution.py:72
  428.9 60.7 %reduce-scatter.11.cloned.1.call-done = bf16[2,64,512]{2,1,0:T(8,128)(2,1)} async-done(((bf16[2,1024,512]{2,1,0:T(8,128)(2,1)}), bf16[2,64,512]{2,1,0:T(8,128)(2,1)}) %reduce-scatter.11.cloned.1.call-update) | async-done | bytes 131088 | tf_op jit(solution)/shard_map/reduce_scatter | solution.py:73
  489.7 7.7 %fusion.8 = f32[1,2,1024,512]{3,2,1,0:T(8,128)} fusion(f32[1,1,1024,512]{3,2,1,0:T(8,128)} %bitcast.77, f32[1,1,1024,512]{3,2,1,0:T(8,128)} %bitcast.75, f32[1,1,1024,512]{3,2,1,0:T(8,128)} %bitcast.73, f32[1,1,1024,512]{3,2,1,0:T(8,128)S(1)} %bitcast.69, f32[1,1,1024,512]{3,2,1,0:T(8,128)} %bitcast.81, f32[1,1,1024,512]{3,2,1,0:T(8,128)} %bitcast.79, ...), kind=kLoop, calls=%fused_computation.18 | loop fusion | flops 9437184 | bytes 20971520 | tf_op jit(solution)/shard_map/add | solution.py:69
  497.3 30.1 %all-gather.2.cloned.1.call-done = bf16[2,1024,512]{2,1,0:T(8,128)(2,1)} async-done(((bf16[2,64,512]{2,1,0:T(8,128)(2,1)}), bf16[2,1024,512]{2,1,0:T(8,128)(2,1)}) %all-gather.2.cloned.1.call-update) | async-done | bytes 2097168 | tf_op jit(solution)/shard_map/all_gather | solution.py:74
  527.5 9.0 %multiply_subtract_fusion = (f32[2,1024,512]{2,1,0:T(8,128)}, f32[2,1024,512]{2,1,0:T(8,128)}) fusion(f32[2,1024,512]{2,1,0:T(8,128)} %param.13, bf16[2,1024,512]{2,1,0:T(8,128)(2,1)} %all-gather.2.cloned.1.call-done, f32[2,1024,512]{2,1,0:T(8,128)} %param.15), kind=kLoop, calls=%fused_computation.19 | loop fusion | flops 6291456 | bytes 18874368 | tf_op jit(solution)/shard_map/sub | solution.py:76
  (66 shorter events, 1.9 us)
Async XLA Ops:
  7.2 3.4 copy-start
  7.2 86.0 %reduce-scatter.5.cloned.1.call-start = ((), (), s32[]{:S(2)}) async-start(), calls=%async_computation.7 | async-start | bytes 1179648 | tf_op jit(solution)/shard_map/reduce_scatter | solution.py:52
  10.5 2.8 copy-start.13
  15.3 1.0 copy-start.19
  16.3 3.3 copy-start.7
  19.4 214.5 %reduce-scatter.7.cloned.1.call-start = ((), (), s32[]{:S(2)}) async-start(), calls=%async_computation.8 | async-start | bytes 1179648 | tf_op jit(solution)/shard_map/reduce_scatter | solution.py:52
  117.2 10.6 %copy-start.10 = (f32[1024,512]{1,0:T(8,128)}, f32[1024,512]{1,0:T(8,128)S(1)}, u32[]{:S(2)}) copy-start(f32[1024,512]{1,0:T(8,128)S(1)} %fusion.16) | copy-start | bytes 6291460
  117.2 3.6 copy-start.2
  120.4 7.3 %copy-start.11 = (f32[1024,512]{1,0:T(8,128)}, f32[1024,512]{1,0:T(8,128)S(1)}, u32[]{:S(2)}) copy-start(f32[1024,512]{1,0:T(8,128)S(1)} %fusion.102) | copy-start | bytes 6291460
  127.8 28.0 %collective-permute-start = (bf16[2,1024,512]{2,1,0:T(8,128)(2,1)}, bf16[2,1024,512]{2,1,0:T(8,128)(2,1)S(1)}, u32[]{:S(2)}, u32[]{:S(2)}) collective-permute-start(bf16[2,1024,512]{2,1,0:T(8,128)(2,1)} %get-tuple-element.11), channel_id=1, source_target_pairs={{120,0},{0,8},{8,16},{16,24},{24,32},{32,40},{40,48},{48,56},{56,6... | collective-permute-start | bytes 6291464 | tf_op jit(solution)/shard_map/ppermute | solution.py:15
  155.8 5.5 %copy-start.6 = (bf16[2,1024,512]{2,1,0:T(8,128)(2,1)}, bf16[2,1024,512]{2,1,0:T(8,128)(2,1)S(1)}, u32[]{:S(2)}) copy-start(bf16[2,1024,512]{2,1,0:T(8,128)(2,1)S(1)} %collective-permute-done) | copy-start | bytes 6291460
  155.8 5.5 %copy-start.16 = (bf16[512,1024]{1,0:T(8,128)(2,1)S(1)}, bf16[512,1024]{1,0:T(8,128)(2,1)}, u32[]{:S(2)}) copy-start(bf16[512,1024]{1,0:T(8,128)(2,1)} %gather_fusion.2) | copy-start | bytes 3145732
  161.3 1.3 copy-start.15
  162.6 1.0 copy-start.21
  163.6 1.9 copy-start.8
  165.4 227.3 %reduce-scatter.9.cloned.1.call-start = ((), (), s32[]{:S(2)}) async-start(), calls=%async_computation.9 | async-start | bytes 1179648 | tf_op jit(solution)/shard_map/reduce_scatter | solution.py:52
  257.9 2.8 copy-start.3
  260.4 5.4 %copy-start.5 = (f32[1024,512]{1,0:T(8,128)}, f32[1024,512]{1,0:T(8,128)S(1)}, u32[]{:S(2)}) copy-start(f32[1024,512]{1,0:T(8,128)S(1)} %fusion.103) | copy-start | bytes 6291460
  265.9 46.1 %collective-permute-start.1 = (bf16[2,1024,512]{2,1,0:T(8,128)(2,1)}, bf16[2,1024,512]{2,1,0:T(8,128)(2,1)}, u32[]{:S(2)}, u32[]{:S(2)}) collective-permute-start(bf16[2,1024,512]{2,1,0:T(8,128)(2,1)} %fusion.105), channel_id=1, source_target_pairs={{112,0},{120,8},{0,16},{8,24},{16,32},{24,40},{32,48},{40,56},{48,... | collective-permute-start | bytes 6291464 | tf_op jit(solution)/shard_map/ppermute | solution.py:15
  270.1 48.2 %copy-start.17 = (bf16[512,1024]{1,0:T(8,128)(2,1)S(1)}, bf16[512,1024]{1,0:T(8,128)(2,1)}, u32[]{:S(2)}) copy-start(bf16[512,1024]{1,0:T(8,128)(2,1)} %gather_fusion.4) | copy-start | bytes 3145732
  318.3 1.3 copy-start.14
  319.6 1.0 copy-start.20
  320.6 2.0 copy-start.9
  322.4 167.2 %reduce-scatter.11.cloned.1.call-start = ((), (), s32[]{:S(2)}) async-start(), calls=%async_computation.10 | async-start | bytes 2228224 | tf_op jit(solution)/shard_map/reduce_scatter | solution.py:73
  412.8 5.3 copy-start.18
  418.2 3.6 copy-start.4
  420.4 1.3 copy-start.12
  428.7 98.8 %all-gather.2.cloned.1.call-start = ((), (), s32[]{:S(2)}) async-start(), calls=%async_computation.11 | async-start | bytes 2228224 | tf_op jit(solution)/shard_map/all_gather | solution.py:74
  527.5 9.0 %copy-start.1 = (bf16[512,1024]{1,0:T(8,128)(2,1)S(1)}, bf16[512,1024]{1,0:T(8,128)(2,1)}, u32[]{:S(2)}) copy-start(bf16[512,1024]{1,0:T(8,128)(2,1)} %param.10) | copy-start | bytes 3145732
Sparse Core Ops, SparseCore 0:
  19.5 73.6 reduce-scatter.4
  165.5 68.3 reduce-scatter.6
  322.5 70.1 reduce-scatter.8
  428.8 60.7 reduce-scatter.10
  491.1 36.2 all-gather.1
